TPU v7x, 256 devices: a whole 4x4x8 slice. The times are simulated.
256 devices in a mesh: row: 32 (over x, y, core), col: 8 (over z).
Axes of the slice: x: 4, y: 4, z: 8, core: 2. Of those that a mesh axis runs over, the one named last changes fastest.
Arguments:
- kernel_tiles: float32 [32, 8, 9, 256, 512], P('row', 'col'), may hold values from -0.09375 to 0.09375
- footprints: int32 [32, 8, 9], P('row', 'col'), may hold values from 0 to 8, as said below
- counts: int32 [32, 8], P('row', 'col'), may hold values from 64 to 256, as said below
- readings: float32 [32, 8, 256], P('row', 'col'), may hold values from -6 to 6
- damping: float32 [1], replicated, may hold values from 0.1 to 0.5
- layer_depth: float32 [2], replicated, may hold values from 1 to 6
- inclinations: float32 [2], replicated, may hold values from 0.6 to 1.3
- declinations: float32 [2], replicated, may hold values from -3.140625 to 3.140625
- resid_grid: float32 [4096, 4096], P('col', 'row'), may hold values from -3 to 3
Outputs:
- coefficients: float32 [32, 8, 512], P('row', 'col')
- rtp_map: float32 [4096, 4096], P(('row', 'col'))
Inputs may be any that keep to these rules, and one draw needn't show every extreme that they name: `footprints`: each tile's list holds each of the 9 codes once; code 3 (a + 1) + (b + 1) names the source block a tiles north and b tiles east of the tile; blocks outside the survey are empty. `counts`: reading slots from this count on are ignored.
All inputs are finite; a program needn't handle non-finite values.
Results may differ from a plain program's by a relative error of at most 0.0003.
Values sent between devices are 32-bit elements; how exact they have to be, the bound alone decides.
A program may use at most 128 MiB of HBM per device.

v0:
```python
import math
import jax
import jax.numpy as jnp
from jax import lax
from jax.sharding import PartitionSpec as P

SRC_ROWS = 8
SRC_COLS = 32
LAYERS = 2
REFINE = 16
INNER_LEN = 128
FOOTPRINT = 9
CG_STEPS = 2
HIGHEST_PRECISION = lax.Precision.HIGHEST
NEIGHBOUR_OFFSETS = tuple(
    ((north_step, east_step) for north_step in (-1, 0, 1) for east_step in (-1, 0, 1))
)


def shifted(x, axis, by):
    peers = lax.axis_size(axis)
    pairs = [(i, i + by) for i in range(peers) if 0 <= i + by < peers]
    return lax.ppermute(x, axis, pairs)


def hat_table(fine_start, fine_count, coarse_start, coarse_count):
    fine_pos = jnp.arange(fine_count, dtype=jnp.float32) + fine_start
    coarse_pos = jnp.arange(coarse_count, dtype=jnp.float32) + coarse_start
    offset = (fine_pos[:, None] + 0.5) / REFINE - 0.5 - coarse_pos[None, :]
    return jnp.maximum(0.0, 1.0 - jnp.abs(offset))


def frequency_of(positions, full_len):
    signed = jnp.where(positions < full_len // 2, positions, positions - full_len)
    return signed.astype(jnp.float32) / full_len


def pole_filter(north_freq, east_freq, inclinations, declinations):
    radius = jnp.sqrt(north_freq * north_freq + east_freq * east_freq)
    safe_radius = jnp.where(radius > 0.0, radius, 1.0)
    unit_north = jnp.where(radius > 0.0, north_freq / safe_radius, 0.0)
    unit_east = jnp.where(radius > 0.0, east_freq / safe_radius, 0.0)
    real_part = jnp.ones_like(radius)
    imag_part = jnp.zeros_like(radius)
    for member in range(2):
        vertical = jnp.sin(inclinations[member])
        horizontal = jnp.cos(inclinations[member])
        along_axis = horizontal * (
            jnp.cos(declinations[member]) * unit_north + jnp.sin(declinations[member]) * unit_east
        )
        denominator = vertical * vertical + along_axis * along_axis
        inv_real = vertical / denominator
        inv_imag = -along_axis / denominator
        real_part, imag_part = (
            real_part * inv_real - imag_part * inv_imag,
            real_part * inv_imag + imag_part * inv_real,
        )
    return (real_part, imag_part)


def phase_table(row_len, col_len, period, direction_sign):
    product = (
        jnp.arange(row_len, dtype=jnp.int32)[:, None]
        * jnp.arange(col_len, dtype=jnp.int32)[None, :]
        % period
    )
    angle = 2.0 * math.pi / period * product.astype(jnp.float32)
    return (jnp.cos(angle), direction_sign * jnp.sin(angle))


def transform_last(real_in, imag_in, direction_sign):
    dims_in = real_in.shape
    length = dims_in[-1]
    outer_len = length // INNER_LEN
    real_blocks = real_in.reshape(-1, outer_len, INNER_LEN)
    cos_outer, sin_outer = phase_table(outer_len, outer_len, outer_len, direction_sign)
    first_real = jnp.einsum("man,ak->mkn", real_blocks, cos_outer, precision=HIGHEST_PRECISION)
    first_imag = jnp.einsum("man,ak->mkn", real_blocks, sin_outer, precision=HIGHEST_PRECISION)
    if imag_in is not None:
        imag_blocks = imag_in.reshape(-1, outer_len, INNER_LEN)
        first_real = first_real - jnp.einsum(
            "man,ak->mkn", imag_blocks, sin_outer, precision=HIGHEST_PRECISION
        )
        first_imag = first_imag + jnp.einsum(
            "man,ak->mkn", imag_blocks, cos_outer, precision=HIGHEST_PRECISION
        )
    twist_cos, twist_sin = phase_table(outer_len, INNER_LEN, length, direction_sign)
    turned_real = first_real * twist_cos - first_imag * twist_sin
    turned_imag = first_real * twist_sin + first_imag * twist_cos
    cos_inner, sin_inner = phase_table(INNER_LEN, INNER_LEN, INNER_LEN, direction_sign)
    final_real = jnp.einsum(
        "mkn,nj->mjk", turned_real, cos_inner, precision=HIGHEST_PRECISION
    ) - jnp.einsum("mkn,nj->mjk", turned_imag, sin_inner, precision=HIGHEST_PRECISION)
    final_imag = jnp.einsum(
        "mkn,nj->mjk", turned_real, sin_inner, precision=HIGHEST_PRECISION
    ) + jnp.einsum("mkn,nj->mjk", turned_imag, cos_inner, precision=HIGHEST_PRECISION)
    return (final_real.reshape(dims_in), final_imag.reshape(dims_in))


def neighbour_block(values, step_by, keep_mask):
    arrived = shifted(values, ("row", "col"), step_by)
    return jnp.where(keep_mask, arrived, 0.0)


def collect_blocks(own_block, col_count, col_index):
    pieces = []
    for north_step, east_step in NEIGHBOUR_OFFSETS:
        if north_step == 0 and east_step == 0:
            pieces.append(own_block)
        else:
            source_col = col_index + east_step
            keep_mask = (source_col >= 0) & (source_col < col_count)
            pieces.append(
                neighbour_block(own_block, -(north_step * col_count + east_step), keep_mask)
            )
    return jnp.stack(pieces)


def return_blocks(spread, col_count, col_index):
    summed = spread[4]
    for position, (north_step, east_step) in enumerate(NEIGHBOUR_OFFSETS):
        if north_step != 0 or east_step != 0:
            source_col = col_index - east_step
            keep_mask = (source_col >= 0) & (source_col < col_count)
            summed = summed + neighbour_block(
                spread[position], north_step * col_count + east_step, keep_mask
            )
    return summed


def local_coarse(solution, col_count, col_index):
    final_blocks = collect_blocks(solution, col_count, col_index)
    coarse = final_blocks.reshape(3, 3, LAYERS, SRC_ROWS, SRC_COLS).transpose(2, 0, 3, 1, 4)
    return coarse.reshape(LAYERS, 3 * SRC_ROWS, 3 * SRC_COLS)


def squares(residual):
    return lax.psum(jnp.sum(residual * residual), ("row", "col"))


def on_device(
    kernel_tiles,
    footprints,
    counts,
    readings,
    damping,
    layer_depth,
    inclinations,
    declinations,
    resid_grid,
):
    col_count = lax.axis_size("col")
    row_count = lax.axis_size("row")
    col_index = lax.axis_index("col")
    row_index = lax.axis_index("row")
    kernels = kernel_tiles[0, 0]
    selector = (
        footprints[0, 0][:, None] == jnp.arange(FOOTPRINT, dtype=jnp.int32)[None, :]
    ).astype(jnp.float32)
    live_mask = (jnp.arange(kernels.shape[1], dtype=jnp.int32) < counts[0, 0]).astype(jnp.float32)
    ridge_weight = damping[0]

    def adjoint(values):
        partial_sums = jnp.einsum(
            "krs,r->ks", kernels, live_mask * values, precision=HIGHEST_PRECISION
        )
        spread = jnp.dot(selector.T, partial_sums, precision=HIGHEST_PRECISION)
        return return_blocks(spread, col_count, col_index)

    right_side = adjoint(readings[0, 0])
    solution = jnp.zeros_like(right_side)
    residual = right_side
    direction = right_side
    norm_now = squares(residual)
    for iteration in range(CG_STEPS):
        blocks = collect_blocks(direction, col_count, col_index)
        chosen = jnp.dot(selector, blocks, precision=HIGHEST_PRECISION)
        applied = (
            adjoint(
                live_mask * jnp.einsum("krs,ks->r", kernels, chosen, precision=HIGHEST_PRECISION)
            )
            + ridge_weight * direction
        )
        step_size = norm_now / lax.psum(jnp.sum(direction * applied), ("row", "col"))
        solution = solution + step_size * direction
        residual = residual - step_size * applied
        if iteration + 1 < CG_STEPS:
            norm_next = squares(residual)
            direction = residual + norm_next / norm_now * direction
            norm_now = norm_next
    tile_east, tile_north = resid_grid.shape
    slab_rows = tile_north // col_count
    coarse = local_coarse(solution, col_count, col_index)
    up_north = hat_table(0.0, tile_north, -float(SRC_ROWS), 3 * SRC_ROWS)
    up_east = hat_table(0.0, tile_east, -float(SRC_COLS), 3 * SRC_COLS)
    eastward = jnp.einsum("lgh,vh->lgv", coarse, up_east, precision=HIGHEST_PRECISION)
    model_planes = jnp.einsum("lgv,ug->lvu", eastward, up_north, precision=HIGHEST_PRECISION)
    tile_planes = jnp.concatenate([model_planes, resid_grid[None]], axis=0)
    planes = lax.all_to_all(tile_planes, "row", split_axis=1, concat_axis=2, tiled=True)
    full_north = planes.shape[-1]
    north_real, north_imag = transform_last(planes, None, -1.0)
    spectra = jnp.stack([north_real, north_imag])
    slab = lax.all_to_all(
        lax.all_to_all(spectra, "row", split_axis=3, concat_axis=2, tiled=True),
        "col",
        split_axis=3,
        concat_axis=2,
        tiled=True,
    )
    slab = jnp.swapaxes(slab, 2, 3)
    full_east = slab.shape[3]
    east_real, east_imag = transform_last(slab[0], slab[1], -1.0)
    north_index = (
        row_index * tile_north + col_index * slab_rows + jnp.arange(slab_rows, dtype=jnp.int32)
    )
    north_freq = frequency_of(north_index, full_north)[:, None]
    east_freq = frequency_of(jnp.arange(full_east, dtype=jnp.int32), full_east)[None, :]
    wavenumber = 2.0 * math.pi * jnp.sqrt(north_freq * north_freq + east_freq * east_freq)
    combined_real = east_real[-1]
    combined_imag = east_imag[-1]
    for layer in range(LAYERS):
        layer_real, layer_imag = (east_real[layer], east_imag[layer])
        damped = jnp.exp(-wavenumber * layer_depth[layer])
        combined_real = combined_real + damped * layer_real
        combined_imag = combined_imag + damped * layer_imag
    filt_real, filt_imag = pole_filter(north_freq, east_freq, inclinations, declinations)
    shaped_real = filt_real * combined_real - filt_imag * combined_imag
    shaped_imag = filt_real * combined_imag + filt_imag * combined_real
    back_real, back_imag = transform_last(shaped_real, shaped_imag, 1.0)
    stacked = jnp.stack([back_real, back_imag]) / full_east
    returned = lax.all_to_all(
        lax.all_to_all(stacked, "row", split_axis=2, concat_axis=1, tiled=True),
        "col",
        split_axis=2,
        concat_axis=1,
        tiled=True,
    )
    returned = jnp.swapaxes(returned, 1, 2)
    out_cols = returned.shape[1]
    ordered = returned.reshape(2, out_cols, col_count, row_count, slab_rows).transpose(
        0, 1, 3, 2, 4
    )
    ordered = ordered.reshape(2, out_cols, full_north)
    final_real, final_imag = transform_last(ordered[0], ordered[1], 1.0)
    rtp_map = final_real / full_north
    return (solution.reshape(1, 1, -1), rtp_map)


def solution(mesh):
    in_specs = (
        P("row", "col", None, None, None),
        P("row", "col", None),
        P("row", "col"),
        P("row", "col", None),
        P(),
        P(),
        P(),
        P(),
        P("col", "row"),
    )
    out_specs = (P("row", "col", None), P(("row", "col"), None))
    return jax.shard_map(
        on_device, mesh=mesh, in_specs=in_specs, out_specs=out_specs, check_vma=False
    )
```

profile of v0, /device:TPU:1, one launch (start us, length us, event | category | flops | bytes accessed | tf_op | source)
XLA Modules:
  0.0 759.6 jit_solution(11323980032133279021)
XLA Ops:
  1.3 4.7 fusion.8
  7.6 5.1 collective-permute-start.1
  14.7 5.0 collective-permute-start.3
  21.6 7.7 %collective-permute-start.5 = (f32[512]{0:T(512)S(1)}, f32[512]{0:T(512)S(1)}, u32[]{:S(2)}, u32[]{:S(2)}) collective-permute-start(f32[512]{0:T(512)S(1)} %bitcast.347), channel_id=1, source_target_pairs={{0,7},{1,8},{2,9},{3,10},{4,11},{5,12},{6,13},{7,14},{8,15},{9,16}... | collective-permute-start | bytes 6152 | tf_op jit(solution)/shard_map/ppermute | solution.py:23
  29.4 5.0 collective-permute-start.6
  36.4 6.2 collective-permute-start.10
  42.6 5.2 collective-permute-start.11
  53.0 5.2 collective-permute-start.8
  67.3 6.2 fusion.6
  87.7 9.0 %collective-permute-start.21 = (f32[512]{0:T(512)S(1)}, f32[512]{0:T(512)S(1)}, u32[]{:S(2)}, u32[]{:S(2)}) collective-permute-start(f32[512]{0:T(512)S(1)} %bitcast.355), channel_id=1, source_target_pairs={{0,7},{1,8},{2,9},{3,10},{4,11},{5,12},{6,13},{7,14},{8,15},{9,16}... | collective-permute-start | bytes 6152 | tf_op jit(solution)/shard_map/ppermute | solution.py:23
  104.6 91.9 %all-reduce = (f32[]{:T(128)}, f32[]{:T(128)}) all-reduce(f32[]{:T(128)} %get-tuple-element.3, f32[]{:T(128)} %get-tuple-element.2), channel_id=1, replica_groups=mesh['row'=32,'col'=8] {'row','col'}, use_global_device_ids=true, to_apply=%region_1.2 | all-reduce | flops 2 | bytes 16 | tf_op jit(solution)/shard_map/psum | solution.py:138
  198.5 74.3 %psum.30 = f32[]{:T(128)} all-reduce(f32[]{:T(128)} %multiply_reduce_fusion.1), channel_id=1, replica_groups=mesh['row'=32,'col'=8] {'row','col'}, use_global_device_ids=true, to_apply=%region_5.6 | all-reduce | flops 1 | bytes 8 | tf_op jit(solution)/shard_map/psum | solution.py:138
  287.1 5.4 collective-permute-start.25
  298.9 6.1 fusion.2
  305.0 4.7 fusion
  315.2 4.7 collective-permute-start.35
  321.8 8.8 %collective-permute-start.37 = (f32[512]{0:T(512)S(1)}, f32[512]{0:T(512)S(1)}, u32[]{:S(2)}, u32[]{:S(2)}) collective-permute-start(f32[512]{0:T(512)S(1)} %bitcast.354), channel_id=1, source_target_pairs={{0,7},{1,8},{2,9},{3,10},{4,11},{5,12},{6,13},{7,14},{8,15},{9,16}... | collective-permute-start | bytes 6152 | tf_op jit(solution)/shard_map/ppermute | solution.py:23
  339.6 86.3 %psum.31 = f32[]{:T(128)} all-reduce(f32[]{:T(128)} %multiply_reduce_fusion), channel_id=1, replica_groups=mesh['row'=32,'col'=8] {'row','col'}, use_global_device_ids=true, to_apply=%region_7.8 | all-reduce | flops 1 | bytes 8 | tf_op jit(solution)/shard_map/psum | solution.py:184
  441.0 4.6 collective-permute-start.41
  455.8 16.3 %all-to-all-start = ((f32[3,512,128]{2,0,1:T(4,128)}), f32[3,512,128]{2,0,1:T(4,128)S(1)}, u32[]{:S(2)}, u32[]{:S(2)}) async-start(f32[3,512,128]{2,0,1:T(4,128)} %copy.161), calls=%async_computation | async-start | bytes 2097152 | tf_op jit(solution)/shard_map/all_to_all | solution.py:199
  472.2 16.7 %all-to-all-done = f32[3,512,128]{2,0,1:T(4,128)S(1)} async-done(((f32[3,512,128]{2,0,1:T(4,128)}), f32[3,512,128]{2,0,1:T(4,128)S(1)}, u32[]{:S(2)}, u32[]{:S(2)}) %all-to-all-start) | async-done | bytes 786464 | tf_op jit(solution)/shard_map/all_to_all | solution.py:199
  511.6 12.5 %copy.169 = f32[2,3,16,4096]{2,0,1,3:T(2,128)} copy(f32[2,3,16,4096]{3,2,1,0:T(8,128)S(1)} %pad_maximum_fusion) | data formatting | bytes 3145728 | tf_op jit(solution)/shard_map/stack | solution.py:202
  524.2 19.0 %reshape.239 = f32[32,1,12288]{2,1,0:T(1,128)S(1)} reshape(f32[4096,3,2,16]{3,2,1,0:T(2,128)} %bitcast.279) | data formatting | bytes 3145728
  543.2 26.6 %all_to_all.87 = f32[32,1,12288]{2,1,0:T(1,128)S(1)} all-to-all(f32[32,1,12288]{2,1,0:T(1,128)S(1)} %reshape.239), channel_id=1, replica_groups=mesh['row'=32,'col'=8] {'row'}, dimensions={0} | all-to-all | bytes 3145728 | tf_op jit(solution)/shard_map/all_to_all | solution.py:204
  574.7 18.7 %reshape.240 = f32[4096,3,2,16]{3,2,1,0:T(2,128)} reshape(f32[32,12288]{1,0:T(8,128)S(1)} %reduce) | data formatting | bytes 3145728
  593.3 14.3 %copy.210 = f32[2,3,16,32,128]{4,2,3,1,0:T(8,128)S(1)} copy(f32[2,3,16,32,128]{2,0,1,4,3:T(2,128)} %bitcast.280) | data formatting | bytes 3145728 | tf_op jit(solution)/shard_map/all_to_all | solution.py:204
  621.2 32.7 %all-to-all-done.2 = f32[2,3,512,128]{2,0,1,3:T(2,128)S(1)} async-done(((f32[2,3,512,128]{2,0,1,3:T(2,128)}), f32[2,3,512,128]{2,0,1,3:T(2,128)S(1)}, u32[]{:S(2)}, u32[]{:S(2)}) %all-to-all-start.2) | async-done | bytes 1572896 | tf_op jit(solution)/shard_map/all_to_all | solution.py:203
  682.3 7.6 reshape.241
  689.8 15.2 %all_to_all.88 = f32[32,1,4096]{2,1,0:T(1,128)S(1)} all-to-all(f32[32,1,4096]{2,1,0:T(1,128)S(1)} %reshape.241), channel_id=1, replica_groups=mesh['row'=32,'col'=8] {'row'}, dimensions={0} | all-to-all | bytes 1048576 | tf_op jit(solution)/shard_map/all_to_all | solution.py:232
  706.9 7.0 reshape.242
  713.8 5.1 copy.212
  719.2 20.9 %all_to_all.89 = f32[2,512,128]{1,0,2:T(2,128)S(1)} all-to-all(f32[2,512,128]{1,0,2:T(2,128)S(1)} %copy.190), channel_id=1, replica_groups=mesh['row'=32,'col'=8] {'col'}, dimensions={2} | all-to-all | bytes 1048576 | tf_op jit(solution)/shard_map/all_to_all | solution.py:231
  (236 shorter events, 187.7 us)
Async XLA Ops:
  6.3 15.3 %collective-permute-start = (f32[512]{0:T(512)S(1)}, f32[512]{0:T(512)S(1)}, u32[]{:S(2)}, u32[]{:S(2)}) collective-permute-start(f32[512]{0:T(512)S(1)} %bitcast.367), channel_id=1, source_target_pairs={{9,0},{10,1},{11,2},{12,3},{13,4},{14,5},{15,6},{16,7},{17,8},{18,... | collective-permute-start | bytes 6152 | tf_op jit(solution)/shard_map/ppermute | solution.py:23
  7.6 21.8 %collective-permute-start.1 = (f32[512]{0:T(512)S(1)}, f32[512]{0:T(512)S(1)}, u32[]{:S(2)}, u32[]{:S(2)}) collective-permute-start(f32[512]{0:T(512)S(1)} %bitcast.364), channel_id=1, source_target_pairs={{8,0},{9,1},{10,2},{11,3},{12,4},{13,5},{14,6},{15,7},{16,8},{17,9... | collective-permute-start | bytes 6152 | tf_op jit(solution)/shard_map/ppermute | solution.py:23
  12.7 21.6 %collective-permute-start.2 = (f32[512]{0:T(512)S(1)}, f32[512]{0:T(512)S(1)}, u32[]{:S(2)}, u32[]{:S(2)}) collective-permute-start(f32[512]{0:T(512)S(1)} %bitcast.361), channel_id=1, source_target_pairs={{7,0},{8,1},{9,2},{10,3},{11,4},{12,5},{13,6},{14,7},{15,8},{16,9}... | collective-permute-start | bytes 6152 | tf_op jit(solution)/shard_map/ppermute | solution.py:23
  14.7 21.0 %collective-permute-start.3 = (f32[512]{0:T(512)S(1)}, f32[512]{0:T(512)S(1)}, u32[]{:S(2)}, u32[]{:S(2)}) collective-permute-start(f32[512]{0:T(512)S(1)} %bitcast.349), channel_id=1, source_target_pairs={{1,0},{2,1},{3,2},{4,3},{5,4},{6,5},{7,6},{8,7},{9,8},{10,9},{11,1... | collective-permute-start | bytes 6152 | tf_op jit(solution)/shard_map/ppermute | solution.py:23
  19.7 16.0 %collective-permute-start.4 = (f32[512]{0:T(512)S(1)}, f32[512]{0:T(512)S(1)}, u32[]{:S(2)}, u32[]{:S(2)}) collective-permute-start(f32[512]{0:T(512)S(1)} %bitcast.348), channel_id=1, source_target_pairs={{0,1},{1,2},{2,3},{3,4},{4,5},{5,6},{6,7},{7,8},{8,9},{9,10},{10,1... | collective-permute-start | bytes 6152 | tf_op jit(solution)/shard_map/ppermute | solution.py:23
  21.6 14.1 %collective-permute-start.5 = (f32[512]{0:T(512)S(1)}, f32[512]{0:T(512)S(1)}, u32[]{:S(2)}, u32[]{:S(2)}) collective-permute-start(f32[512]{0:T(512)S(1)} %bitcast.347), channel_id=1, source_target_pairs={{0,7},{1,8},{2,9},{3,10},{4,11},{5,12},{6,13},{7,14},{8,15},{9,16}... | collective-permute-start | bytes 6152 | tf_op jit(solution)/shard_map/ppermute | solution.py:23
  36.4 16.6 %collective-permute-start.10 = (f32[512]{0:T(512)S(1)}, f32[512]{0:T(512)S(1)}, u32[]{:S(2)}, u32[]{:S(2)}) collective-permute-start(f32[512]{0:T(512)S(1)} %select_add_fusion.1), channel_id=1, source_target_pairs={{0,7},{1,8},{2,9},{3,10},{4,11},{5,12},{6,13},{7,14},{8,15},{9,16}... | collective-permute-start | bytes 6152 | tf_op jit(solution)/shard_map/ppermute | solution.py:23
  42.6 15.6 %collective-permute-start.11 = (f32[512]{0:T(512)S(1)}, f32[512]{0:T(512)S(1)}, u32[]{:S(2)}, u32[]{:S(2)}) collective-permute-start(f32[512]{0:T(512)S(1)} %select_add_fusion.1), channel_id=1, source_target_pairs={{0,1},{1,2},{2,3},{3,4},{4,5},{5,6},{6,7},{7,8},{8,9},{9,10},{10,1... | collective-permute-start | bytes 6152 | tf_op jit(solution)/shard_map/ppermute | solution.py:23
  47.8 14.3 %collective-permute-start.12 = (f32[512]{0:T(512)S(1)}, f32[512]{0:T(512)S(1)}, u32[]{:S(2)}, u32[]{:S(2)}) collective-permute-start(f32[512]{0:T(512)S(1)} %select_add_fusion.1), channel_id=1, source_target_pairs={{1,0},{2,1},{3,2},{4,3},{5,4},{6,5},{7,6},{8,7},{9,8},{10,9},{11,1... | collective-permute-start | bytes 6152 | tf_op jit(solution)/shard_map/ppermute | solution.py:23
  49.7 14.3 %collective-permute-start.13 = (f32[512]{0:T(512)S(1)}, f32[512]{0:T(512)S(1)}, u32[]{:S(2)}, u32[]{:S(2)}) collective-permute-start(f32[512]{0:T(512)S(1)} %select_add_fusion.1), channel_id=1, source_target_pairs={{7,0},{8,1},{9,2},{10,3},{11,4},{12,5},{13,6},{14,7},{15,8},{16,9}... | collective-permute-start | bytes 6152 | tf_op jit(solution)/shard_map/ppermute | solution.py:23
  51.7 12.4 %collective-permute-start.15 = (f32[512]{0:T(512)S(1)}, f32[512]{0:T(512)S(1)}, u32[]{:S(2)}, u32[]{:S(2)}) collective-permute-start(f32[512]{0:T(512)S(1)} %select_add_fusion.1), channel_id=1, source_target_pairs={{9,0},{10,1},{11,2},{12,3},{13,4},{14,5},{15,6},{16,7},{17,8},{18,... | collective-permute-start | bytes 6152 | tf_op jit(solution)/shard_map/ppermute | solution.py:23
  77.5 19.2 %collective-permute-start.17 = (f32[512]{0:T(512)S(1)}, f32[512]{0:T(512)S(1)}, u32[]{:S(2)}, u32[]{:S(2)}) collective-permute-start(f32[512]{0:T(512)S(1)} %bitcast.365), channel_id=1, source_target_pairs={{8,0},{9,1},{10,2},{11,3},{12,4},{13,5},{14,6},{15,7},{16,8},{17,9... | collective-permute-start | bytes 6152 | tf_op jit(solution)/shard_map/ppermute | solution.py:23
  79.4 21.0 %collective-permute-start.18 = (f32[512]{0:T(512)S(1)}, f32[512]{0:T(512)S(1)}, u32[]{:S(2)}, u32[]{:S(2)}) collective-permute-start(f32[512]{0:T(512)S(1)} %bitcast.362), channel_id=1, source_target_pairs={{7,0},{8,1},{9,2},{10,3},{11,4},{12,5},{13,6},{14,7},{15,8},{16,9}... | collective-permute-start | bytes 6152 | tf_op jit(solution)/shard_map/ppermute | solution.py:23
  81.3 22.6 %collective-permute-start.19 = (f32[512]{0:T(512)S(1)}, f32[512]{0:T(512)S(1)}, u32[]{:S(2)}, u32[]{:S(2)}) collective-permute-start(f32[512]{0:T(512)S(1)} %bitcast.359), channel_id=1, source_target_pairs={{1,0},{2,1},{3,2},{4,3},{5,4},{6,5},{7,6},{8,7},{9,8},{10,9},{11,1... | collective-permute-start | bytes 6152 | tf_op jit(solution)/shard_map/ppermute | solution.py:23
  85.8 18.2 %collective-permute-start.20 = (f32[512]{0:T(512)S(1)}, f32[512]{0:T(512)S(1)}, u32[]{:S(2)}, u32[]{:S(2)}) collective-permute-start(f32[512]{0:T(512)S(1)} %bitcast.357), channel_id=1, source_target_pairs={{0,1},{1,2},{2,3},{3,4},{4,5},{5,6},{6,7},{7,8},{8,9},{9,10},{10,1... | collective-permute-start | bytes 6152 | tf_op jit(solution)/shard_map/ppermute | solution.py:23
  87.7 16.2 %collective-permute-start.21 = (f32[512]{0:T(512)S(1)}, f32[512]{0:T(512)S(1)}, u32[]{:S(2)}, u32[]{:S(2)}) collective-permute-start(f32[512]{0:T(512)S(1)} %bitcast.355), channel_id=1, source_target_pairs={{0,7},{1,8},{2,9},{3,10},{4,11},{5,12},{6,13},{7,14},{8,15},{9,16}... | collective-permute-start | bytes 6152 | tf_op jit(solution)/shard_map/ppermute | solution.py:23
  274.2 12.9 %collective-permute-start.26 = (f32[512]{0:T(512)S(1)}, f32[512]{0:T(512)S(1)}, u32[]{:S(2)}, u32[]{:S(2)}) collective-permute-start(f32[512]{0:T(512)S(1)} %multiply_add_fusion.12), channel_id=1, source_target_pairs={{0,7},{1,8},{2,9},{3,10},{4,11},{5,12},{6,13},{7,14},{8,15},{9,16}... | collective-permute-start | bytes 6152 | tf_op jit(solution)/shard_map/ppermute | solution.py:23
  276.9 15.6 %collective-permute-start.27 = (f32[512]{0:T(512)S(1)}, f32[512]{0:T(512)S(1)}, u32[]{:S(2)}, u32[]{:S(2)}) collective-permute-start(f32[512]{0:T(512)S(1)} %multiply_add_fusion.12), channel_id=1, source_target_pairs={{0,1},{1,2},{2,3},{3,4},{4,5},{5,6},{6,7},{7,8},{8,9},{9,10},{10,1... | collective-permute-start | bytes 6152 | tf_op jit(solution)/shard_map/ppermute | solution.py:23
  280.8 13.7 %collective-permute-start.28 = (f32[512]{0:T(512)S(1)}, f32[512]{0:T(512)S(1)}, u32[]{:S(2)}, u32[]{:S(2)}) collective-permute-start(f32[512]{0:T(512)S(1)} %multiply_add_fusion.12), channel_id=1, source_target_pairs={{1,0},{2,1},{3,2},{4,3},{5,4},{6,5},{7,6},{8,7},{9,8},{10,9},{11,1... | collective-permute-start | bytes 6152 | tf_op jit(solution)/shard_map/ppermute | solution.py:23
  283.7 14.3 %collective-permute-start.29 = (f32[512]{0:T(512)S(1)}, f32[512]{0:T(512)S(1)}, u32[]{:S(2)}, u32[]{:S(2)}) collective-permute-start(f32[512]{0:T(512)S(1)} %multiply_add_fusion.12), channel_id=1, source_target_pairs={{7,0},{8,1},{9,2},{10,3},{11,4},{12,5},{13,6},{14,7},{15,8},{16,9}... | collective-permute-start | bytes 6152 | tf_op jit(solution)/shard_map/ppermute | solution.py:23
  285.6 12.3 %collective-permute-start.31 = (f32[512]{0:T(512)S(1)}, f32[512]{0:T(512)S(1)}, u32[]{:S(2)}, u32[]{:S(2)}) collective-permute-start(f32[512]{0:T(512)S(1)} %multiply_add_fusion.12), channel_id=1, source_target_pairs={{9,0},{10,1},{11,2},{12,3},{13,4},{14,5},{15,6},{16,7},{17,8},{18,... | collective-permute-start | bytes 6152 | tf_op jit(solution)/shard_map/ppermute | solution.py:23
  311.3 19.3 %collective-permute-start.33 = (f32[512]{0:T(512)S(1)}, f32[512]{0:T(512)S(1)}, u32[]{:S(2)}, u32[]{:S(2)}) collective-permute-start(f32[512]{0:T(512)S(1)} %bitcast.363), channel_id=1, source_target_pairs={{8,0},{9,1},{10,2},{11,3},{12,4},{13,5},{14,6},{15,7},{16,8},{17,9... | collective-permute-start | bytes 6152 | tf_op jit(solution)/shard_map/ppermute | solution.py:23
  313.2 21.6 %collective-permute-start.34 = (f32[512]{0:T(512)S(1)}, f32[512]{0:T(512)S(1)}, u32[]{:S(2)}, u32[]{:S(2)}) collective-permute-start(f32[512]{0:T(512)S(1)} %bitcast.360), channel_id=1, source_target_pairs={{7,0},{8,1},{9,2},{10,3},{11,4},{12,5},{13,6},{14,7},{15,8},{16,9}... | collective-permute-start | bytes 6152 | tf_op jit(solution)/shard_map/ppermute | solution.py:23
  315.2 23.1 %collective-permute-start.35 = (f32[512]{0:T(512)S(1)}, f32[512]{0:T(512)S(1)}, u32[]{:S(2)}, u32[]{:S(2)}) collective-permute-start(f32[512]{0:T(512)S(1)} %bitcast.358), channel_id=1, source_target_pairs={{1,0},{2,1},{3,2},{4,3},{5,4},{6,5},{7,6},{8,7},{9,8},{10,9},{11,1... | collective-permute-start | bytes 6152 | tf_op jit(solution)/shard_map/ppermute | solution.py:23
  319.9 18.4 %collective-permute-start.36 = (f32[512]{0:T(512)S(1)}, f32[512]{0:T(512)S(1)}, u32[]{:S(2)}, u32[]{:S(2)}) collective-permute-start(f32[512]{0:T(512)S(1)} %bitcast.356), channel_id=1, source_target_pairs={{0,1},{1,2},{2,3},{3,4},{4,5},{5,6},{6,7},{7,8},{8,9},{9,10},{10,1... | collective-permute-start | bytes 6152 | tf_op jit(solution)/shard_map/ppermute | solution.py:23
  321.8 16.5 %collective-permute-start.37 = (f32[512]{0:T(512)S(1)}, f32[512]{0:T(512)S(1)}, u32[]{:S(2)}, u32[]{:S(2)}) collective-permute-start(f32[512]{0:T(512)S(1)} %bitcast.354), channel_id=1, source_target_pairs={{0,7},{1,8},{2,9},{3,10},{4,11},{5,12},{6,13},{7,14},{8,15},{9,16}... | collective-permute-start | bytes 6152 | tf_op jit(solution)/shard_map/ppermute | solution.py:23
  427.2 13.7 %collective-permute-start.42 = (f32[512]{0:T(512)S(1)}, f32[512]{0:T(512)S(1)}, u32[]{:S(2)}, u32[]{:S(2)}) collective-permute-start(f32[512]{0:T(512)S(1)} %multiply_add_fusion.11), channel_id=1, source_target_pairs={{0,7},{1,8},{2,9},{3,10},{4,11},{5,12},{6,13},{7,14},{8,15},{9,16}... | collective-permute-start | bytes 6152 | tf_op jit(solution)/shard_map/ppermute | solution.py:23
  430.9 14.7 %collective-permute-start.43 = (f32[512]{0:T(512)S(1)}, f32[512]{0:T(512)S(1)}, u32[]{:S(2)}, u32[]{:S(2)}) collective-permute-start(f32[512]{0:T(512)S(1)} %multiply_add_fusion.11), channel_id=1, source_target_pairs={{0,1},{1,2},{2,3},{3,4},{4,5},{5,6},{6,7},{7,8},{8,9},{9,10},{10,1... | collective-permute-start | bytes 6152 | tf_op jit(solution)/shard_map/ppermute | solution.py:23
  433.1 14.4 %collective-permute-start.44 = (f32[512]{0:T(512)S(1)}, f32[512]{0:T(512)S(1)}, u32[]{:S(2)}, u32[]{:S(2)}) collective-permute-start(f32[512]{0:T(512)S(1)} %multiply_add_fusion.11), channel_id=1, source_target_pairs={{1,0},{2,1},{3,2},{4,3},{5,4},{6,5},{7,6},{8,7},{9,8},{10,9},{11,1... | collective-permute-start | bytes 6152 | tf_op jit(solution)/shard_map/ppermute | solution.py:23
  437.7 14.1 %collective-permute-start.45 = (f32[512]{0:T(512)S(1)}, f32[512]{0:T(512)S(1)}, u32[]{:S(2)}, u32[]{:S(2)}) collective-permute-start(f32[512]{0:T(512)S(1)} %multiply_add_fusion.11), channel_id=1, source_target_pairs={{7,0},{8,1},{9,2},{10,3},{11,4},{12,5},{13,6},{14,7},{15,8},{16,9}... | collective-permute-start | bytes 6152 | tf_op jit(solution)/shard_map/ppermute | solution.py:23
  455.8 33.1 %all-to-all-start = ((f32[3,512,128]{2,0,1:T(4,128)}), f32[3,512,128]{2,0,1:T(4,128)S(1)}, u32[]{:S(2)}, u32[]{:S(2)}) async-start(f32[3,512,128]{2,0,1:T(4,128)} %copy.161), calls=%async_computation | async-start | bytes 2097152 | tf_op jit(solution)/shard_map/all_to_all | solution.py:199
  609.9 44.0 %all-to-all-start.2 = ((f32[2,3,512,128]{2,0,1,3:T(2,128)}), f32[2,3,512,128]{2,0,1,3:T(2,128)S(1)}, u32[]{:S(2)}, u32[]{:S(2)}) async-start(f32[2,3,512,128]{2,0,1,3:T(2,128)} %copy.172), calls=%async_computation.2 | async-start | bytes 3145728 | tf_op jit(solution)/shard_map/all_to_all | solution.py:203
  (26 other events, 384.7 us)
where the time goes:
time: 771 us; the launch traced here: 760 us
  blocking collectives  315 us (41%)
  starting transfers between devices  180 us (23%)
  local copies, waits for them, and re-layouts  123 us (16%)
  matrix products  61.8 us (8%)
  waiting for transfers between devices  55 us (7%)
  between operations  13.2 us (2%)
  other arithmetic  11.7 us (2%)
    psum x2, blocking collectives, squares(): return lax.psum(jnp.sum(residual * residual), ('row', 'col'))  166 us
    ppermute x48, starting transfers between devices, shifted(): return lax.ppermute(x, axis, pairs)  160 us
    psum x1, blocking collectives, on_device(): lax.psum(jnp.sum(direction * applied), ('row', 'col'))  86.3 us
    unnamed x22, local copies, waits for them, and re-layouts  52.5 us
    all_to_all x1, waiting for transfers between devices, on_device(): lax.all_to_all(lax.all_to_all(spectra, 'row', split_axis=3, concat_axis=2...  32.7 us
    all_to_all x1, blocking collectives, on_device(): lax.all_to_all(spectra, 'row', split_axis=3, concat_axis=2, tiled=True)  26.6 us
    all_to_all x1, blocking collectives, on_device(): lax.all_to_all(lax.all_to_all(stacked, 'row', split_axis=2, concat_axis=1...  20.9 us
    another operation x3, local copies, waits for them, and re-layouts, on_device(): spectra = jnp.stack([north_real, north_imag])  17.2 us
  transfers between devices with their start and end apart: 50, of which 7 were waited for; matrix products, arithmetic and copies ran while one was open for 0% of the time, Pallas kernels for 0%

commit v1 on v0

--- a/solution.py
+++ b/solution.py
@@ -229,7 +229,12 @@
     back_real, back_imag = transform_last(shaped_real, shaped_imag, 1.0)
     stacked = jnp.stack([back_real, back_imag]) / full_east
     returned = lax.all_to_all(
-        lax.all_to_all(stacked, "row", split_axis=2, concat_axis=1, tiled=True),
+        jnp.concatenate(
+            lax.all_to_all(
+                jnp.stack(jnp.split(stacked, lax.axis_size("row"), axis=2)), "row", 0, 0
+            ),
+            axis=1,
+        ),
         "col",
         split_axis=2,
         concat_axis=1,

time: 771 us -> 745 us (0.966)
  local copies, waits for them, and re-layouts: 123 us -> 98.7 us
    unnamed x22 -> x51, local copies, waits for them, and re-layouts: 52.5 us -> 38.1 us
where the time goes in v1:
time: 745 us; the launch traced here: 734 us
  blocking collectives  315 us (42%)
  starting transfers between devices  181 us (24%)
  local copies, waits for them, and re-layouts  98.7 us (13%)
  matrix products  61.8 us (8%)
  waiting for transfers between devices  54.4 us (7%)
  between operations  13.8 us (2%)
  other arithmetic  9.91 us (1%)
    psum x2, blocking collectives, squares(): return lax.psum(jnp.sum(residual * residual), ('row', 'col'))  166 us
    ppermute x48, starting transfers between devices, shifted(): return lax.ppermute(x, axis, pairs)  160 us
    psum x1, blocking collectives, on_device(): lax.psum(jnp.sum(direction * applied), ('row', 'col'))  86.3 us
    unnamed x51, local copies, waits for them, and re-layouts  38.1 us
    all_to_all x1, waiting for transfers between devices, on_device(): lax.all_to_all(lax.all_to_all(spectra, 'row', split_axis=3, concat_axis=2...  32.1 us
    all_to_all x1, blocking collectives, on_device(): lax.all_to_all(spectra, 'row', split_axis=3, concat_axis=2, tiled=True)  26.6 us
    all_to_all x1, blocking collectives, on_device(): lax.all_to_all(jnp.concatenate(lax.all_to_all(jnp.stack(jnp.split(stacked...  20.6 us
    another operation x3, local copies, waits for them, and re-layouts, on_device(): spectra = jnp.stack([north_real, north_imag])  17.2 us
  transfers between devices with their start and end apart: 50, of which 7 were waited for; matrix products, arithmetic and copies ran while one was open for 0% of the time, Pallas kernels for 0%

profile of v1, /device:TPU:1, one launch (start us, length us, event | category | flops | bytes accessed | tf_op | source)
XLA Modules:
  0.0 734.1 jit_solution(11216628166609211613)
XLA Ops:
  1.3 4.7 fusion.8
  7.6 5.1 collective-permute-start.1
  14.7 5.0 collective-permute-start.3
  21.6 7.7 %collective-permute-start.5 = (f32[512]{0:T(512)S(1)}, f32[512]{0:T(512)S(1)}, u32[]{:S(2)}, u32[]{:S(2)}) collective-permute-start(f32[512]{0:T(512)S(1)} %bitcast.469), channel_id=1, source_target_pairs={{0,7},{1,8},{2,9},{3,10},{4,11},{5,12},{6,13},{7,14},{8,15},{9,16}... | collective-permute-start | bytes 6152 | tf_op jit(solution)/shard_map/ppermute | solution.py:23
  29.4 5.0 collective-permute-start.6
  36.4 6.2 collective-permute-start.10
  42.6 5.2 collective-permute-start.11
  53.0 5.2 collective-permute-start.8
  67.3 6.2 fusion.6
  81.3 4.4 collective-permute-start.19
  87.7 9.0 %collective-permute-start.21 = (f32[512]{0:T(512)S(1)}, f32[512]{0:T(512)S(1)}, u32[]{:S(2)}, u32[]{:S(2)}) collective-permute-start(f32[512]{0:T(512)S(1)} %bitcast.477), channel_id=1, source_target_pairs={{0,7},{1,8},{2,9},{3,10},{4,11},{5,12},{6,13},{7,14},{8,15},{9,16}... | collective-permute-start | bytes 6152 | tf_op jit(solution)/shard_map/ppermute | solution.py:23
  104.7 91.9 %all-reduce = (f32[]{:T(128)}, f32[]{:T(128)}) all-reduce(f32[]{:T(128)} %get-tuple-element.3, f32[]{:T(128)} %get-tuple-element.2), channel_id=1, replica_groups=mesh['row'=32,'col'=8] {'row','col'}, use_global_device_ids=true, to_apply=%region_1.2 | all-reduce | flops 2 | bytes 16 | tf_op jit(solution)/shard_map/psum | solution.py:138
  198.5 74.3 %psum.30 = f32[]{:T(128)} all-reduce(f32[]{:T(128)} %multiply_reduce_fusion.1), channel_id=1, replica_groups=mesh['row'=32,'col'=8] {'row','col'}, use_global_device_ids=true, to_apply=%region_5.6 | all-reduce | flops 1 | bytes 8 | tf_op jit(solution)/shard_map/psum | solution.py:138
  287.4 5.4 collective-permute-start.25
  299.2 6.1 fusion.2
  305.3 4.7 fusion
  315.5 4.7 collective-permute-start.35
  322.1 8.8 %collective-permute-start.37 = (f32[512]{0:T(512)S(1)}, f32[512]{0:T(512)S(1)}, u32[]{:S(2)}, u32[]{:S(2)}) collective-permute-start(f32[512]{0:T(512)S(1)} %bitcast.476), channel_id=1, source_target_pairs={{0,7},{1,8},{2,9},{3,10},{4,11},{5,12},{6,13},{7,14},{8,15},{9,16}... | collective-permute-start | bytes 6152 | tf_op jit(solution)/shard_map/ppermute | solution.py:23
  339.9 86.3 %psum.31 = f32[]{:T(128)} all-reduce(f32[]{:T(128)} %multiply_reduce_fusion), channel_id=1, replica_groups=mesh['row'=32,'col'=8] {'row','col'}, use_global_device_ids=true, to_apply=%region_7.8 | all-reduce | flops 1 | bytes 8 | tf_op jit(solution)/shard_map/psum | solution.py:184
  433.4 4.6 collective-permute-start.44
  441.2 4.6 collective-permute-start.41
  456.0 16.3 %all-to-all-start = ((f32[3,512,128]{2,0,1:T(4,128)}), f32[3,512,128]{2,0,1:T(4,128)S(1)}, u32[]{:S(2)}, u32[]{:S(2)}) async-start(f32[3,512,128]{2,0,1:T(4,128)} %copy.159), calls=%async_computation | async-start | bytes 2097152 | tf_op jit(solution)/shard_map/all_to_all | solution.py:199
  472.4 16.7 %all-to-all-done = f32[3,512,128]{2,0,1:T(4,128)S(1)} async-done(((f32[3,512,128]{2,0,1:T(4,128)}), f32[3,512,128]{2,0,1:T(4,128)S(1)}, u32[]{:S(2)}, u32[]{:S(2)}) %all-to-all-start) | async-done | bytes 786464 | tf_op jit(solution)/shard_map/all_to_all | solution.py:199
  511.6 12.6 %copy.167 = f32[2,3,16,4096]{2,0,1,3:T(2,128)} copy(f32[2,3,16,4096]{3,2,1,0:T(8,128)S(1)} %pad_maximum_fusion) | data formatting | bytes 3145728 | tf_op jit(solution)/shard_map/stack | solution.py:202
  524.2 19.0 %reshape.247 = f32[32,1,12288]{2,1,0:T(1,128)S(1)} reshape(f32[4096,3,2,16]{3,2,1,0:T(2,128)} %bitcast.402) | data formatting | bytes 3145728
  543.2 26.6 %all_to_all.74 = f32[32,1,12288]{2,1,0:T(1,128)S(1)} all-to-all(f32[32,1,12288]{2,1,0:T(1,128)S(1)} %reshape.247), channel_id=1, replica_groups=mesh['row'=32,'col'=8] {'row'}, dimensions={0} | all-to-all | bytes 3145728 | tf_op jit(solution)/shard_map/all_to_all | solution.py:204
  570.3 4.4 reduce
  574.7 18.7 %reshape.248 = f32[4096,3,2,16]{3,2,1,0:T(2,128)} reshape(f32[32,12288]{1,0:T(8,128)S(1)} %reduce) | data formatting | bytes 3145728
  593.4 14.3 %copy.206 = f32[2,3,16,32,128]{4,2,3,1,0:T(8,128)S(1)} copy(f32[2,3,16,32,128]{2,0,1,4,3:T(2,128)} %bitcast.403) | data formatting | bytes 3145728 | tf_op jit(solution)/shard_map/all_to_all | solution.py:204
  621.8 32.1 %all-to-all-done.2 = f32[2,3,512,128]{2,0,1,3:T(2,128)S(1)} async-done(((f32[2,3,512,128]{2,0,1,3:T(2,128)}), f32[2,3,512,128]{2,0,1,3:T(2,128)S(1)}, u32[]{:S(2)}, u32[]{:S(2)}) %all-to-all-start.2) | async-done | bytes 1572896 | tf_op jit(solution)/shard_map/all_to_all | solution.py:203
  678.4 15.2 %all_to_all.75 = f32[32,2,16,128]{3,2,1,0:T(8,128)S(1)} all-to-all(f32[32,2,16,128]{3,2,1,0:T(8,128)S(1)} %constant_dynamic-update-slice_fusion), channel_id=1, replica_groups=mesh['row'=32,'col'=8] {'row'}, dimensions={0} | all-to-all | bytes 1048576 | tf_op jit(solution)/shard_map/all_to_all | solution.py:233
  693.9 20.6 %all_to_all.76 = f32[2,512,128]{1,0,2:T(2,128)S(1)} all-to-all(f32[2,512,128]{1,0,2:T(2,128)S(1)} %copy.186), channel_id=1, replica_groups=mesh['row'=32,'col'=8] {'col'}, dimensions={2} | all-to-all | bytes 1048576 | tf_op jit(solution)/shard_map/all_to_all | solution.py:231
  (264 shorter events, 168.7 us)
Async XLA Ops:
  6.3 15.3 %collective-permute-start = (f32[512]{0:T(512)S(1)}, f32[512]{0:T(512)S(1)}, u32[]{:S(2)}, u32[]{:S(2)}) collective-permute-start(f32[512]{0:T(512)S(1)} %bitcast.489), channel_id=1, source_target_pairs={{9,0},{10,1},{11,2},{12,3},{13,4},{14,5},{15,6},{16,7},{17,8},{18,... | collective-permute-start | bytes 6152 | tf_op jit(solution)/shard_map/ppermute | solution.py:23
  7.6 21.8 %collective-permute-start.1 = (f32[512]{0:T(512)S(1)}, f32[512]{0:T(512)S(1)}, u32[]{:S(2)}, u32[]{:S(2)}) collective-permute-start(f32[512]{0:T(512)S(1)} %bitcast.486), channel_id=1, source_target_pairs={{8,0},{9,1},{10,2},{11,3},{12,4},{13,5},{14,6},{15,7},{16,8},{17,9... | collective-permute-start | bytes 6152 | tf_op jit(solution)/shard_map/ppermute | solution.py:23
  12.7 21.6 %collective-permute-start.2 = (f32[512]{0:T(512)S(1)}, f32[512]{0:T(512)S(1)}, u32[]{:S(2)}, u32[]{:S(2)}) collective-permute-start(f32[512]{0:T(512)S(1)} %bitcast.483), channel_id=1, source_target_pairs={{7,0},{8,1},{9,2},{10,3},{11,4},{12,5},{13,6},{14,7},{15,8},{16,9}... | collective-permute-start | bytes 6152 | tf_op jit(solution)/shard_map/ppermute | solution.py:23
  14.7 21.0 %collective-permute-start.3 = (f32[512]{0:T(512)S(1)}, f32[512]{0:T(512)S(1)}, u32[]{:S(2)}, u32[]{:S(2)}) collective-permute-start(f32[512]{0:T(512)S(1)} %bitcast.471), channel_id=1, source_target_pairs={{1,0},{2,1},{3,2},{4,3},{5,4},{6,5},{7,6},{8,7},{9,8},{10,9},{11,1... | collective-permute-start | bytes 6152 | tf_op jit(solution)/shard_map/ppermute | solution.py:23
  19.7 16.0 %collective-permute-start.4 = (f32[512]{0:T(512)S(1)}, f32[512]{0:T(512)S(1)}, u32[]{:S(2)}, u32[]{:S(2)}) collective-permute-start(f32[512]{0:T(512)S(1)} %bitcast.470), channel_id=1, source_target_pairs={{0,1},{1,2},{2,3},{3,4},{4,5},{5,6},{6,7},{7,8},{8,9},{9,10},{10,1... | collective-permute-start | bytes 6152 | tf_op jit(solution)/shard_map/ppermute | solution.py:23
  21.6 14.1 %collective-permute-start.5 = (f32[512]{0:T(512)S(1)}, f32[512]{0:T(512)S(1)}, u32[]{:S(2)}, u32[]{:S(2)}) collective-permute-start(f32[512]{0:T(512)S(1)} %bitcast.469), channel_id=1, source_target_pairs={{0,7},{1,8},{2,9},{3,10},{4,11},{5,12},{6,13},{7,14},{8,15},{9,16}... | collective-permute-start | bytes 6152 | tf_op jit(solution)/shard_map/ppermute | solution.py:23
  36.4 16.6 %collective-permute-start.10 = (f32[512]{0:T(512)S(1)}, f32[512]{0:T(512)S(1)}, u32[]{:S(2)}, u32[]{:S(2)}) collective-permute-start(f32[512]{0:T(512)S(1)} %select_add_fusion.1), channel_id=1, source_target_pairs={{0,7},{1,8},{2,9},{3,10},{4,11},{5,12},{6,13},{7,14},{8,15},{9,16}... | collective-permute-start | bytes 6152 | tf_op jit(solution)/shard_map/ppermute | solution.py:23
  42.6 15.6 %collective-permute-start.11 = (f32[512]{0:T(512)S(1)}, f32[512]{0:T(512)S(1)}, u32[]{:S(2)}, u32[]{:S(2)}) collective-permute-start(f32[512]{0:T(512)S(1)} %select_add_fusion.1), channel_id=1, source_target_pairs={{0,1},{1,2},{2,3},{3,4},{4,5},{5,6},{6,7},{7,8},{8,9},{9,10},{10,1... | collective-permute-start | bytes 6152 | tf_op jit(solution)/shard_map/ppermute | solution.py:23
  47.8 14.3 %collective-permute-start.12 = (f32[512]{0:T(512)S(1)}, f32[512]{0:T(512)S(1)}, u32[]{:S(2)}, u32[]{:S(2)}) collective-permute-start(f32[512]{0:T(512)S(1)} %select_add_fusion.1), channel_id=1, source_target_pairs={{1,0},{2,1},{3,2},{4,3},{5,4},{6,5},{7,6},{8,7},{9,8},{10,9},{11,1... | collective-permute-start | bytes 6152 | tf_op jit(solution)/shard_map/ppermute | solution.py:23
  49.7 14.3 %collective-permute-start.13 = (f32[512]{0:T(512)S(1)}, f32[512]{0:T(512)S(1)}, u32[]{:S(2)}, u32[]{:S(2)}) collective-permute-start(f32[512]{0:T(512)S(1)} %select_add_fusion.1), channel_id=1, source_target_pairs={{7,0},{8,1},{9,2},{10,3},{11,4},{12,5},{13,6},{14,7},{15,8},{16,9}... | collective-permute-start | bytes 6152 | tf_op jit(solution)/shard_map/ppermute | solution.py:23
  51.7 12.4 %collective-permute-start.15 = (f32[512]{0:T(512)S(1)}, f32[512]{0:T(512)S(1)}, u32[]{:S(2)}, u32[]{:S(2)}) collective-permute-start(f32[512]{0:T(512)S(1)} %select_add_fusion.1), channel_id=1, source_target_pairs={{9,0},{10,1},{11,2},{12,3},{13,4},{14,5},{15,6},{16,7},{17,8},{18,... | collective-permute-start | bytes 6152 | tf_op jit(solution)/shard_map/ppermute | solution.py:23
  77.5 19.2 %collective-permute-start.17 = (f32[512]{0:T(512)S(1)}, f32[512]{0:T(512)S(1)}, u32[]{:S(2)}, u32[]{:S(2)}) collective-permute-start(f32[512]{0:T(512)S(1)} %bitcast.487), channel_id=1, source_target_pairs={{8,0},{9,1},{10,2},{11,3},{12,4},{13,5},{14,6},{15,7},{16,8},{17,9... | collective-permute-start | bytes 6152 | tf_op jit(solution)/shard_map/ppermute | solution.py:23
  79.4 21.0 %collective-permute-start.18 = (f32[512]{0:T(512)S(1)}, f32[512]{0:T(512)S(1)}, u32[]{:S(2)}, u32[]{:S(2)}) collective-permute-start(f32[512]{0:T(512)S(1)} %bitcast.484), channel_id=1, source_target_pairs={{7,0},{8,1},{9,2},{10,3},{11,4},{12,5},{13,6},{14,7},{15,8},{16,9}... | collective-permute-start | bytes 6152 | tf_op jit(solution)/shard_map/ppermute | solution.py:23
  81.3 22.6 %collective-permute-start.19 = (f32[512]{0:T(512)S(1)}, f32[512]{0:T(512)S(1)}, u32[]{:S(2)}, u32[]{:S(2)}) collective-permute-start(f32[512]{0:T(512)S(1)} %bitcast.481), channel_id=1, source_target_pairs={{1,0},{2,1},{3,2},{4,3},{5,4},{6,5},{7,6},{8,7},{9,8},{10,9},{11,1... | collective-permute-start | bytes 6152 | tf_op jit(solution)/shard_map/ppermute | solution.py:23
  85.8 18.2 %collective-permute-start.20 = (f32[512]{0:T(512)S(1)}, f32[512]{0:T(512)S(1)}, u32[]{:S(2)}, u32[]{:S(2)}) collective-permute-start(f32[512]{0:T(512)S(1)} %bitcast.479), channel_id=1, source_target_pairs={{0,1},{1,2},{2,3},{3,4},{4,5},{5,6},{6,7},{7,8},{8,9},{9,10},{10,1... | collective-permute-start | bytes 6152 | tf_op jit(solution)/shard_map/ppermute | solution.py:23
  87.7 16.2 %collective-permute-start.21 = (f32[512]{0:T(512)S(1)}, f32[512]{0:T(512)S(1)}, u32[]{:S(2)}, u32[]{:S(2)}) collective-permute-start(f32[512]{0:T(512)S(1)} %bitcast.477), channel_id=1, source_target_pairs={{0,7},{1,8},{2,9},{3,10},{4,11},{5,12},{6,13},{7,14},{8,15},{9,16}... | collective-permute-start | bytes 6152 | tf_op jit(solution)/shard_map/ppermute | solution.py:23
  274.2 13.2 %collective-permute-start.26 = (f32[512]{0:T(512)S(1)}, f32[512]{0:T(512)S(1)}, u32[]{:S(2)}, u32[]{:S(2)}) collective-permute-start(f32[512]{0:T(512)S(1)} %multiply_add_fusion.12), channel_id=1, source_target_pairs={{0,7},{1,8},{2,9},{3,10},{4,11},{5,12},{6,13},{7,14},{8,15},{9,16}... | collective-permute-start | bytes 6152 | tf_op jit(solution)/shard_map/ppermute | solution.py:23
  276.9 15.9 %collective-permute-start.27 = (f32[512]{0:T(512)S(1)}, f32[512]{0:T(512)S(1)}, u32[]{:S(2)}, u32[]{:S(2)}) collective-permute-start(f32[512]{0:T(512)S(1)} %multiply_add_fusion.12), channel_id=1, source_target_pairs={{0,1},{1,2},{2,3},{3,4},{4,5},{5,6},{6,7},{7,8},{8,9},{9,10},{10,1... | collective-permute-start | bytes 6152 | tf_op jit(solution)/shard_map/ppermute | solution.py:23
  280.8 14.0 %collective-permute-start.28 = (f32[512]{0:T(512)S(1)}, f32[512]{0:T(512)S(1)}, u32[]{:S(2)}, u32[]{:S(2)}) collective-permute-start(f32[512]{0:T(512)S(1)} %multiply_add_fusion.12), channel_id=1, source_target_pairs={{1,0},{2,1},{3,2},{4,3},{5,4},{6,5},{7,6},{8,7},{9,8},{10,9},{11,1... | collective-permute-start | bytes 6152 | tf_op jit(solution)/shard_map/ppermute | solution.py:23
  283.7 14.5 %collective-permute-start.29 = (f32[512]{0:T(512)S(1)}, f32[512]{0:T(512)S(1)}, u32[]{:S(2)}, u32[]{:S(2)}) collective-permute-start(f32[512]{0:T(512)S(1)} %multiply_add_fusion.12), channel_id=1, source_target_pairs={{7,0},{8,1},{9,2},{10,3},{11,4},{12,5},{13,6},{14,7},{15,8},{16,9}... | collective-permute-start | bytes 6152 | tf_op jit(solution)/shard_map/ppermute | solution.py:23
  285.6 12.6 %collective-permute-start.31 = (f32[512]{0:T(512)S(1)}, f32[512]{0:T(512)S(1)}, u32[]{:S(2)}, u32[]{:S(2)}) collective-permute-start(f32[512]{0:T(512)S(1)} %multiply_add_fusion.12), channel_id=1, source_target_pairs={{9,0},{10,1},{11,2},{12,3},{13,4},{14,5},{15,6},{16,7},{17,8},{18,... | collective-permute-start | bytes 6152 | tf_op jit(solution)/shard_map/ppermute | solution.py:23
  311.6 19.3 %collective-permute-start.33 = (f32[512]{0:T(512)S(1)}, f32[512]{0:T(512)S(1)}, u32[]{:S(2)}, u32[]{:S(2)}) collective-permute-start(f32[512]{0:T(512)S(1)} %bitcast.485), channel_id=1, source_target_pairs={{8,0},{9,1},{10,2},{11,3},{12,4},{13,5},{14,6},{15,7},{16,8},{17,9... | collective-permute-start | bytes 6152 | tf_op jit(solution)/shard_map/ppermute | solution.py:23
  313.5 21.6 %collective-permute-start.34 = (f32[512]{0:T(512)S(1)}, f32[512]{0:T(512)S(1)}, u32[]{:S(2)}, u32[]{:S(2)}) collective-permute-start(f32[512]{0:T(512)S(1)} %bitcast.482), channel_id=1, source_target_pairs={{7,0},{8,1},{9,2},{10,3},{11,4},{12,5},{13,6},{14,7},{15,8},{16,9}... | collective-permute-start | bytes 6152 | tf_op jit(solution)/shard_map/ppermute | solution.py:23
  315.5 23.1 %collective-permute-start.35 = (f32[512]{0:T(512)S(1)}, f32[512]{0:T(512)S(1)}, u32[]{:S(2)}, u32[]{:S(2)}) collective-permute-start(f32[512]{0:T(512)S(1)} %bitcast.480), channel_id=1, source_target_pairs={{1,0},{2,1},{3,2},{4,3},{5,4},{6,5},{7,6},{8,7},{9,8},{10,9},{11,1... | collective-permute-start | bytes 6152 | tf_op jit(solution)/shard_map/ppermute | solution.py:23
  320.2 18.4 %collective-permute-start.36 = (f32[512]{0:T(512)S(1)}, f32[512]{0:T(512)S(1)}, u32[]{:S(2)}, u32[]{:S(2)}) collective-permute-start(f32[512]{0:T(512)S(1)} %bitcast.478), channel_id=1, source_target_pairs={{0,1},{1,2},{2,3},{3,4},{4,5},{5,6},{6,7},{7,8},{8,9},{9,10},{10,1... | collective-permute-start | bytes 6152 | tf_op jit(solution)/shard_map/ppermute | solution.py:23
  322.1 16.5 %collective-permute-start.37 = (f32[512]{0:T(512)S(1)}, f32[512]{0:T(512)S(1)}, u32[]{:S(2)}, u32[]{:S(2)}) collective-permute-start(f32[512]{0:T(512)S(1)} %bitcast.476), channel_id=1, source_target_pairs={{0,7},{1,8},{2,9},{3,10},{4,11},{5,12},{6,13},{7,14},{8,15},{9,16}... | collective-permute-start | bytes 6152 | tf_op jit(solution)/shard_map/ppermute | solution.py:23
  427.5 13.7 %collective-permute-start.42 = (f32[512]{0:T(512)S(1)}, f32[512]{0:T(512)S(1)}, u32[]{:S(2)}, u32[]{:S(2)}) collective-permute-start(f32[512]{0:T(512)S(1)} %multiply_add_fusion.11), channel_id=1, source_target_pairs={{0,7},{1,8},{2,9},{3,10},{4,11},{5,12},{6,13},{7,14},{8,15},{9,16}... | collective-permute-start | bytes 6152 | tf_op jit(solution)/shard_map/ppermute | solution.py:23
  431.2 14.7 %collective-permute-start.43 = (f32[512]{0:T(512)S(1)}, f32[512]{0:T(512)S(1)}, u32[]{:S(2)}, u32[]{:S(2)}) collective-permute-start(f32[512]{0:T(512)S(1)} %multiply_add_fusion.11), channel_id=1, source_target_pairs={{0,1},{1,2},{2,3},{3,4},{4,5},{5,6},{6,7},{7,8},{8,9},{9,10},{10,1... | collective-permute-start | bytes 6152 | tf_op jit(solution)/shard_map/ppermute | solution.py:23
  433.4 14.4 %collective-permute-start.44 = (f32[512]{0:T(512)S(1)}, f32[512]{0:T(512)S(1)}, u32[]{:S(2)}, u32[]{:S(2)}) collective-permute-start(f32[512]{0:T(512)S(1)} %multiply_add_fusion.11), channel_id=1, source_target_pairs={{1,0},{2,1},{3,2},{4,3},{5,4},{6,5},{7,6},{8,7},{9,8},{10,9},{11,1... | collective-permute-start | bytes 6152 | tf_op jit(solution)/shard_map/ppermute | solution.py:23
  438.0 14.1 %collective-permute-start.45 = (f32[512]{0:T(512)S(1)}, f32[512]{0:T(512)S(1)}, u32[]{:S(2)}, u32[]{:S(2)}) collective-permute-start(f32[512]{0:T(512)S(1)} %multiply_add_fusion.11), channel_id=1, source_target_pairs={{7,0},{8,1},{9,2},{10,3},{11,4},{12,5},{13,6},{14,7},{15,8},{16,9}... | collective-permute-start | bytes 6152 | tf_op jit(solution)/shard_map/ppermute | solution.py:23
  456.0 33.1 %all-to-all-start = ((f32[3,512,128]{2,0,1:T(4,128)}), f32[3,512,128]{2,0,1:T(4,128)S(1)}, u32[]{:S(2)}, u32[]{:S(2)}) async-start(f32[3,512,128]{2,0,1:T(4,128)} %copy.159), calls=%async_computation | async-start | bytes 2097152 | tf_op jit(solution)/shard_map/all_to_all | solution.py:199
  609.9 44.0 %all-to-all-start.2 = ((f32[2,3,512,128]{2,0,1,3:T(2,128)}), f32[2,3,512,128]{2,0,1,3:T(2,128)S(1)}, u32[]{:S(2)}, u32[]{:S(2)}) async-start(f32[2,3,512,128]{2,0,1,3:T(2,128)} %copy.170), calls=%async_computation.2 | async-start | bytes 3145728 | tf_op jit(solution)/shard_map/all_to_all | solution.py:203
  (26 other events, 385.7 us)
